TPU v7x, 512 devices: a whole 4x8x8 slice. The times are simulated.
512 devices in a mesh: seq: 16 (over y_lo, z), clus: 32 (over x, y_hi, core).
Axes of the slice: x: 4, y: 8 (y_hi: 4, y_lo: 2; y = y_hi * 2 + y_lo), z: 8, core: 2. Of those that a mesh axis runs over, the one named last changes fastest.
Arguments:
- node_feats: bfloat16 [32, 2048, 1024], P('clus', 'seq'), may hold values from -24 to 24
- qkv_weight: bfloat16 [3072, 1024], P('seq'), may hold values from -1 to 1
- block_pairs: int32 [32, 128, 2], P('clus'), may hold values from 0 to 15, as said below
- grad_out: bfloat16 [32, 2048, 1024], P('clus', 'seq'), may hold values from -6 to 6
Outputs:
- attended: bfloat16 [32, 2048, 1024], P('clus', 'seq')
- node_grad: bfloat16 [32, 2048, 1024], P('clus', 'seq')
- weight_grad: float32 [3072, 1024], P('seq')
Inputs may be any that keep to these rules, and one draw needn't show every extreme that they name: `block_pairs`: each cluster's list holds 128 distinct pairs, among them (b, b) for every block b.
All inputs are finite; a program needn't handle non-finite values.
Results may differ from a plain program's by a relative error of at most 0.023.
Values may be sent and summed in bfloat16 or wider, within the bound.
A program may use at most 64 MiB of HBM per device.

v0:
```python
import math
import jax
import jax.numpy as jnp
from jax import lax
from jax.sharding import PartitionSpec as P

HD = 64
BLOCK = 128


def block_allowed(listed, blocks):
    block_ids = jnp.arange(blocks, dtype=jnp.int32)[None, :]
    row_hot = (listed[:, 0:1] == block_ids).astype(jnp.float32)
    col_hot = (listed[:, 1:2] == block_ids).astype(jnp.float32)
    counts = jnp.dot(row_hot.T, col_hot, precision=lax.Precision.HIGHEST)
    return counts > 0.5


def expand_rows(allowed_blocks, offset, row_span):
    picked = lax.dynamic_slice_in_dim(allowed_blocks, offset // BLOCK, row_span // BLOCK, 0)
    return jnp.repeat(jnp.repeat(picked, BLOCK, axis=0), BLOCK, axis=1)


def softmax_rows(query_rows, keys_all, allowed_rows):
    scores = jnp.einsum(
        "qhe,khe->hqk", query_rows, keys_all, preferred_element_type=jnp.float32
    ) * HD ** (-0.5)
    scores = jnp.where(allowed_rows[None], scores, -jnp.inf)
    row_max = jnp.max(scores, axis=-1, keepdims=True)
    unnorm = jnp.where(allowed_rows[None], jnp.exp(scores - row_max), 0.0)
    return unnorm / jnp.sum(unnorm, axis=-1, keepdims=True)


def local(node_feats, qkv_weight, block_pairs, grad_out):
    features = node_feats[0]
    rows_dev = features.shape[0]
    node_count = rows_dev * lax.axis_size("seq")
    columns = qkv_weight.shape[0]
    heads_dev = columns // (3 * HD)
    row_span = math.gcd(node_count, 512)
    offsets = jnp.arange(node_count // row_span, dtype=jnp.int32) * row_span
    projected = lax.dot_general(
        lax.all_gather(features, "seq", axis=0, tiled=True),
        qkv_weight,
        (((1,), (1,)), ((), ())),
        preferred_element_type=jnp.float32,
    ).astype(jnp.bfloat16)
    grouped = projected.reshape(node_count, heads_dev, 3, HD)
    queries = grouped[:, :, 0]
    keys_all = grouped[:, :, 1]
    values_all = grouped[:, :, 2]
    allowed_blocks = block_allowed(block_pairs[0], node_count // BLOCK)

    def forward_block(offset):
        query_rows = lax.dynamic_slice_in_dim(queries, offset, row_span, 0)
        weights = softmax_rows(query_rows, keys_all, expand_rows(allowed_blocks, offset, row_span))
        return jnp.einsum(
            "hqk,khe->qhe",
            weights.astype(jnp.bfloat16),
            values_all,
            preferred_element_type=jnp.float32,
        ).astype(jnp.bfloat16)

    head_out = lax.map(forward_block, offsets).reshape(node_count, heads_dev * HD)
    attended = lax.all_to_all(head_out, "seq", split_axis=0, concat_axis=1, tiled=True)
    upstream = lax.all_to_all(grad_out[0], "seq", split_axis=1, concat_axis=0, tiled=True).reshape(
        node_count, heads_dev, HD
    )

    def backward_block(state_pair, offset):
        grad_keys, grad_values = state_pair
        query_rows = lax.dynamic_slice_in_dim(queries, offset, row_span, 0)
        grad_rows = lax.dynamic_slice_in_dim(upstream, offset, row_span, 0)
        weights = softmax_rows(query_rows, keys_all, expand_rows(allowed_blocks, offset, row_span))
        weights_low = weights.astype(jnp.bfloat16)
        grad_weights = jnp.einsum(
            "qhe,khe->hqk", grad_rows, values_all, preferred_element_type=jnp.float32
        )
        row_delta = jnp.sum(weights * grad_weights, axis=-1, keepdims=True)
        grad_scores = (weights * (grad_weights - row_delta) * HD ** (-0.5)).astype(jnp.bfloat16)
        grad_query = jnp.einsum(
            "hqk,khe->qhe", grad_scores, keys_all, preferred_element_type=jnp.float32
        ).astype(jnp.bfloat16)
        grad_keys = grad_keys + jnp.einsum(
            "hqk,qhe->khe", grad_scores, query_rows, preferred_element_type=jnp.float32
        )
        grad_values = grad_values + jnp.einsum(
            "hqk,qhe->khe", weights_low, grad_rows, preferred_element_type=jnp.float32
        )
        return ((grad_keys, grad_values), grad_query)

    zeros_acc = jnp.zeros((node_count, heads_dev, HD), jnp.float32)
    sums_pair, grad_query = lax.scan(backward_block, (zeros_acc, zeros_acc), offsets)
    grad_query = grad_query.reshape(node_count, heads_dev, HD)
    grad_proj = jnp.stack(
        [grad_query, sums_pair[0].astype(jnp.bfloat16), sums_pair[1].astype(jnp.bfloat16)], axis=2
    ).reshape(node_count, columns)
    rows_part = grad_proj
    node_grad = lax.psum_scatter(
        jnp.dot(rows_part, qkv_weight, preferred_element_type=jnp.float32).astype(jnp.bfloat16),
        "seq",
        scatter_dimension=0,
        tiled=True,
    )
    rows_part = grad_proj
    local_sum = lax.dot_general(
        rows_part,
        lax.all_gather(features, "seq", axis=0, tiled=True),
        (((0,), (0,)), ((), ())),
        preferred_element_type=jnp.float32,
    )
    weight_grad = lax.psum(local_sum.astype(jnp.bfloat16), "clus").astype(
        jnp.float32
    ) / lax.axis_size("clus")
    return (attended[None], node_grad[None], weight_grad)


def solution(mesh):
    return jax.shard_map(
        local,
        mesh=mesh,
        in_specs=(
            P("clus", "seq", None),
            P("seq", None),
            P("clus", None, None),
            P("clus", "seq", None),
        ),
        out_specs=(P("clus", "seq", None), P("clus", "seq", None), P("seq", None)),
        check_vma=False,
    )
```

profile of v0, /device:TPU:6, one launch (start us, length us, event | category | flops | bytes accessed | tf_op | source)
XLA Modules:
  0.0 562.7 jit_solution(15509004296155294109)
XLA Ops:
  7.9 1.8 copy.19
  9.7 11.4 %all-to-all-start.1 = ((bf16[128,16,64]{0,2,1:T(8,128)(2,1)}), bf16[128,16,64]{0,2,1:T(8,128)(2,1)S(1)}, u32[]{:S(2)}, u32[]{:S(2)}) async-start(bf16[128,16,64]{0,2,1:T(8,128)(2,1)} %bitcast.19), calls=%async_computation.1 | async-start | bytes 524288 | tf_op jit(solution)/shard_map/all_to_all | solution.py:66
  22.2 9.6 %all-to-all-done.1 = bf16[128,16,64]{0,2,1:T(8,128)(2,1)S(1)} async-done(((bf16[128,16,64]{0,2,1:T(8,128)(2,1)}), bf16[128,16,64]{0,2,1:T(8,128)(2,1)S(1)}, u32[]{:S(2)}, u32[]{:S(2)}) %all-to-all-start.1) | async-done | bytes 262176 | tf_op jit(solution)/shard_map/all_to_all | solution.py:66
  32.8 61.0 %all-gather.3.cloned.1.call-done = bf16[1,2048,1024]{2,1,0:T(8,128)(2,1)} async-done(((bf16[1,128,1024]{2,1,0:T(8,128)(2,1)}), bf16[1,2048,1024]{2,1,0:T(8,128)(2,1)}) %all-gather.3.cloned.1.call-update) | async-done | bytes 4194320 | tf_op jit(solution)/shard_map/all_gather | solution.py:43
  93.8 3.7 fusion.44
  99.2 88.3 %while.30 = (s32[]{:T(128)}, f32[2048,1,64]{0,2,1:T(8,128)S(1)}, f32[2048,1,64]{0,2,1:T(8,128)S(1)}, bf16[4,512,1,64]{1,3,2,0:T(8,128)(2,1)}, s32[4]{0:T(128)S(1...) while((s32[]{:T(128)}, f32[2048,1,64]{0,2,1:T(8,128)S(1)}, ...), condition=%wide.region_8.9_spmd.clone, body=%wide.region_4.8_spmd.clone.sunk | while | flops 692615680 | bytes 80837776 | solution.py:93
  102.1 3.5 broadcast_in_dim.122
  106.7 2.2 fusion.84
  110.2 3.0 multiply_reduce_fusion.2
  113.3 2.0 copy-done.1
  115.8 1.6 fusion.86
  117.4 2.4 fusion.88
  124.2 3.5 broadcast_in_dim.122
  128.8 2.2 fusion.84
  132.3 3.0 multiply_reduce_fusion.2
  135.4 2.0 copy-done.1
  137.9 1.6 fusion.86
  139.5 2.4 fusion.88
  146.3 3.5 broadcast_in_dim.122
  150.9 2.2 fusion.84
  154.4 3.0 multiply_reduce_fusion.2
  157.5 2.0 copy-done.1
  160.0 1.6 fusion.86
  161.6 2.4 fusion.88
  168.4 3.5 broadcast_in_dim.122
  173.0 2.2 fusion.84
  176.5 3.0 multiply_reduce_fusion.2
  179.6 2.0 copy-done.1
  183.7 2.4 fusion.88
  189.0 3.9 fusion.47
  193.2 3.2 convolution_convert_fusion.1
  196.5 56.6 %while.29 = (s32[]{:T(128)}, bf16[4,512,1,64]{1,3,2,0:T(8,128)(2,1)S(1)}, s32[4]{0:T(128)S(1)}, pred[16,16]{1,0:T(8,128)(4,1)S(1)}, bf16[2048,1,64]{0,2,1:T(8,12...) while((s32[]{:T(128)}, ...), condition=%wide.region_3.4_spmd, body=%wide.region_0.3_spmd.sunk | while | flops 283147264 | bytes 17459756 | solution.py:64
  199.8 3.5 broadcast_in_dim.117
  204.5 2.2 fusion.75
  208.1 2.6 fusion.77
  213.9 3.5 broadcast_in_dim.117
  218.7 2.2 fusion.75
  222.2 2.6 fusion.77
  228.1 3.5 broadcast_in_dim.117
  232.8 2.2 fusion.75
  236.4 2.6 fusion.77
  242.2 3.5 broadcast_in_dim.117
  247.0 2.2 fusion.75
  250.5 2.6 fusion.77
  254.2 3.9 all-to-all-start
  258.1 203.0 %all-reduce.2.cloned.1.call-done = bf16[192,1024]{1,0:T(8,128)(2,1)} async-done(((bf16[192,1024]{1,0:T(8,128)(2,1)}), bf16[192,1024]{1,0:T(8,128)(2,1)}) %all-reduce.2.cloned.1.call-update) | async-done | bytes 393232 | tf_op jit(solution)/shard_map/psum | solution.py:112
  461.1 2.0 convert_multiply_fusion
  463.9 92.3 %reduce-scatter.2.cloned.1.call-done = bf16[128,1024]{1,0:T(8,128)(2,1)} async-done(((bf16[2048,1024]{1,0:T(8,128)(2,1)}), bf16[128,1024]{1,0:T(8,128)(2,1)}) %reduce-scatter.2.cloned.1.call-update) | async-done | bytes 262160 | tf_op jit(solution)/shard_map/reduce_scatter | solution.py:99
  (80 shorter events, 34.2 us)
Async XLA Ops:
  7.2 86.7 %copy-start = (bf16[192,1024]{1,0:T(8,128)(2,1)S(1)}, bf16[192,1024]{1,0:T(8,128)(2,1)}, u32[]{:S(2)}) copy-start(bf16[192,1024]{1,0:T(8,128)(2,1)} %param.9) | copy-start | bytes 1179652
  7.2 86.7 %all-gather.3.cloned.1.call-start = ((), (), s32[]{:S(2)}) async-start(), calls=%async_computation.5 | async-start | bytes 4456448 | tf_op jit(solution)/shard_map/all_gather | solution.py:43
  9.7 22.1 %all-to-all-start.1 = ((bf16[128,16,64]{0,2,1:T(8,128)(2,1)}), bf16[128,16,64]{0,2,1:T(8,128)(2,1)S(1)}, u32[]{:S(2)}, u32[]{:S(2)}) async-start(bf16[128,16,64]{0,2,1:T(8,128)(2,1)} %bitcast.19), calls=%async_computation.1 | async-start | bytes 524288 | tf_op jit(solution)/shard_map/all_to_all | solution.py:66
  21.1 439.9 %all-reduce.2.cloned.1.call-start = ((), (), s32[]{:S(2)}) async-start(), calls=%async_computation.4 | async-start | bytes 786432 | tf_op jit(solution)/shard_map/psum | solution.py:112
  113.3 2.0 copy-start.1
  115.8 4.0 copy-start.2
  135.4 2.0 copy-start.1
  137.9 4.0 copy-start.2
  157.5 2.0 copy-start.1
  160.0 4.0 copy-start.2
  179.6 2.0 copy-start.1
  182.1 4.0 copy-start.2
  192.9 363.3 %reduce-scatter.2.cloned.1.call-start = ((), (), s32[]{:S(2)}) async-start(), calls=%async_computation.3 | async-start | bytes 4456448 | tf_op jit(solution)/shard_map/reduce_scatter | solution.py:99
  254.2 208.8 %all-to-all-start = ((bf16[16,128,64]{1,2,0:T(8,128)(2,1)}), bf16[16,128,64]{1,2,0:T(8,128)(2,1)S(1)}, u32[]{:S(2)}, u32[]{:S(2)}) async-start(bf16[16,128,64]{1,2,0:T(8,128)(2,1)} %copy.18), calls=%async_computation | async-start | bytes 524288 | tf_op jit(solution)/shard_map/all_to_all | solution.py:65
Sparse Core Ops, SparseCore 0:
  10.1 83.7 all-gather.2
  193.1 267.9 all-reduce.1
  464.5 91.6 reduce-scatter.1
where the time goes:
time: 564 us; the launch traced here: 563 us
  waiting for transfers between devices  367 us (65%)
  matrix products  72.6 us (13%)
  local copies, waits for them, and re-layouts  49.3 us (9%)
  loops' own time  29.3 us (5%)
  starting transfers between devices  15.6 us (3%)
  other arithmetic  15.5 us (3%)
  between operations  13.9 us (2%)
    psum x1, waiting for transfers between devices, local(): lax.psum(local_sum.astype(jnp.bfloat16), 'clus').astype(jnp.float32)  203 us
    reduce_scatter x1, waiting for transfers between devices, local(): lax.psum_scatter(jnp.dot(rows_part, qkv_weight, preferred_element_type=jn...  92.3 us
    all_gather x1, waiting for transfers between devices, local(): lax.all_gather(features, 'seq', axis=0, tiled=True)  61 us
    broadcast_in_dim x16, local copies, waits for them, and re-layouts, expand_rows(): return jnp.repeat(jnp.repeat(picked, BLOCK, axis=0), BLOCK, axis=1)  27.9 us
    dot_general x8, matrix products, softmax_rows(): jnp.einsum('qhe,khe->hqk', query_rows, keys_all, preferred_element_type=j...  17.3 us
    another operation x1, loops' own time, local(): lax.map(forward_block, offsets).reshape(node_count, heads_dev * HD)  15.5 us
    another operation x1, loops' own time, local(): lax.scan(backward_block, (zeros_acc, zeros_acc), offsets)  13.8 us
    dot_general x4, matrix products, backward_block(): jnp.einsum('qhe,khe->hqk', grad_rows, values_all, preferred_element_type=...  12.1 us
  transfers between devices with their start and end apart: 5, of which 4 were waited for; matrix products, arithmetic and copies ran while one was open for 9% of the time, Pallas kernels for 0%

commit v1 on v0

--- a/solution.py
+++ b/solution.py
@@ -40,7 +40,9 @@
     row_span = math.gcd(node_count, 512)
     offsets = jnp.arange(node_count // row_span, dtype=jnp.int32) * row_span
     projected = lax.dot_general(
-        lax.all_gather(features, "seq", axis=0, tiled=True),
+        jnp.concatenate(
+            lax.all_to_all(jnp.stack([features] * lax.axis_size("seq")), "seq", 0, 0), axis=0
+        ),
         qkv_weight,
         (((1,), (1,)), ((), ())),
         preferred_element_type=jnp.float32,

time: 564 us -> 632 us (1.12)
  waiting for transfers between devices: 367 us -> 417 us
  blocking collectives: 0 us -> 21.9 us
    all_to_all x1, waiting for transfers between devices: 9.6 us -> 120 us  [local(): lax.all_to_all(jnp.stack([features] * lax.axis_size('seq')), 'seq', 0, 0)]
    all_gather x1, waiting for transfers between devices: 61 us -> 0.02 us  [local(): lax.all_gather(features, 'seq', axis=0, tiled=True)]
    all_to_all x0 -> x1, blocking collectives: none -> 21.9 us  [local(): lax.all_to_all(grad_out[0], 'seq', split_axis=1, concat_axis=0, tiled=True)]
    all_to_all x1, starting transfers between devices: 11.4 us -> 4.67 us  [local(): lax.all_to_all(jnp.stack([features] * lax.axis_size('seq')), 'seq', 0, 0)]
  transfers between devices with their start and end apart: 5 -> 5, of which waited for: 4 -> 3; matrix products, arithmetic and copies ran while one was open for 9% -> 19% of each run, Pallas kernels for 0% -> 0%
where the time goes in v1:
time: 632 us; the launch traced here: 631 us
  waiting for transfers between devices  417 us (66%)
  matrix products  72.6 us (11%)
  local copies, waits for them, and re-layouts  51.1 us (8%)
  loops' own time  29 us (5%)
  blocking collectives  21.9 us (3%)
  other arithmetic  15.5 us (2%)
  between operations  13.9 us (2%)
  starting transfers between devices  9.79 us (2%)
    psum x1, waiting for transfers between devices, local(): lax.psum(local_sum.astype(jnp.bfloat16), 'clus').astype(jnp.float32)  205 us
    all_to_all x1, waiting for transfers between devices, local(): lax.all_to_all(jnp.stack([features] * lax.axis_size('seq')), 'seq', 0, 0)  120 us
    reduce_scatter x1, waiting for transfers between devices, local(): lax.psum_scatter(jnp.dot(rows_part, qkv_weight, preferred_element_type=jn...  92.3 us
    broadcast_in_dim x16, local copies, waits for them, and re-layouts, expand_rows(): return jnp.repeat(jnp.repeat(picked, BLOCK, axis=0), BLOCK, axis=1)  27.9 us
    all_to_all x1, blocking collectives, local(): lax.all_to_all(grad_out[0], 'seq', split_axis=1, concat_axis=0, tiled=True)  21.9 us
    dot_general x8, matrix products, softmax_rows(): jnp.einsum('qhe,khe->hqk', query_rows, keys_all, preferred_element_type=j...  17.3 us
    another operation x1, loops' own time, local(): lax.map(forward_block, offsets).reshape(node_count, heads_dev * HD)  15.4 us
    another operation x1, loops' own time, local(): lax.scan(backward_block, (zeros_acc, zeros_acc), offsets)  13.6 us
  transfers between devices with their start and end apart: 5, of which 3 were waited for; matrix products, arithmetic and copies ran while one was open for 19% of the time, Pallas kernels for 0%

profile of v1, /device:TPU:6, one launch (start us, length us, event | category | flops | bytes accessed | tf_op | source)
XLA Modules:
  0.0 631.0 jit_solution(126770877168843011)
XLA Ops:
  8.4 21.9 %all_to_all.37 = bf16[128,16,64]{0,2,1:T(8,128)(2,1)S(1)} all-to-all(bf16[128,16,64]{0,2,1:T(8,128)(2,1)S(1)} %bitcast.217), channel_id=1, replica_groups=mesh['seq'=16,'clus'=32] {'seq'}, dimensions={1} | all-to-all | bytes 524288 | tf_op jit(solution)/shard_map/all_to_all | solution.py:68
  30.3 3.4 stack.12
  33.7 4.7 all-to-all-start
  40.5 119.7 %all-to-all-done = bf16[16,128,1024]{2,1,0:T(8,128)(2,1)} async-done(((bf16[16,128,1024]{2,1,0:T(8,128)(2,1)}), bf16[16,128,1024]{2,1,0:T(8,128)(2,1)}, u32[]{:S(2)}, u32[]{:S(2)}) %all-to-all-start) | async-done | bytes 4194336 | tf_op jit(solution)/shard_map/all_to_all | solution.py:44
  160.2 3.7 convolution_convert_fusion.2
  165.6 88.0 %while.30 = (s32[]{:T(128)}, f32[2048,1,64]{0,2,1:T(8,128)S(1)}, f32[2048,1,64]{0,2,1:T(8,128)S(1)}, bf16[4,512,1,64]{1,3,2,0:T(8,128)(2,1)}, s32[4]{0:T(128)S(1...) while((s32[]{:T(128)}, f32[2048,1,64]{0,2,1:T(8,128)S(1)}, ...), condition=%wide.region_8.9_spmd.clone, body=%wide.region_4.8_spmd.clone.sunk | while | flops 692615680 | bytes 80837776 | solution.py:95
  168.4 3.5 broadcast_in_dim.122
  172.9 2.2 fusion.80
  176.5 3.0 multiply_reduce_fusion.2
  179.6 2.0 copy-done.1
  182.1 1.6 fusion.82
  183.7 2.4 fusion.84
  190.4 3.5 broadcast_in_dim.122
  195.0 2.2 fusion.80
  198.5 3.0 multiply_reduce_fusion.2
  201.6 2.0 copy-done.1
  204.1 1.6 fusion.82
  205.7 2.4 fusion.84
  212.4 3.5 broadcast_in_dim.122
  217.0 2.2 fusion.80
  220.5 3.0 multiply_reduce_fusion.2
  223.6 2.0 copy-done.1
  226.1 1.6 fusion.82
  227.8 2.4 fusion.84
  234.4 3.5 broadcast_in_dim.122
  239.0 2.2 fusion.80
  242.6 3.0 multiply_reduce_fusion.2
  245.6 2.0 copy-done.1
  249.7 2.4 fusion.84
  255.1 3.9 fusion.42
  259.2 3.2 convolution_convert_fusion.1
  262.5 56.4 %while.29 = (s32[]{:T(128)}, bf16[4,512,1,64]{1,3,2,0:T(8,128)(2,1)S(1)}, s32[4]{0:T(128)S(1)}, pred[16,16]{1,0:T(8,128)(4,1)S(1)}, bf16[2048,1,64]{0,2,1:T(8,12...) while((s32[]{:T(128)}, ...), condition=%wide.region_3.4_spmd, body=%wide.region_0.3_spmd.sunk | while | flops 283147264 | bytes 17459756 | solution.py:66
  265.7 3.5 broadcast_in_dim.117
  270.5 2.2 fusion.71
  274.0 2.6 fusion.73
  279.8 3.5 broadcast_in_dim.117
  284.6 2.2 fusion.71
  288.1 2.6 fusion.73
  294.0 3.5 broadcast_in_dim.117
  298.7 2.2 fusion.71
  302.3 2.6 fusion.73
  308.1 3.5 broadcast_in_dim.117
  312.8 2.2 fusion.71
  316.4 2.6 fusion.73
  320.0 4.8 all-to-all-start.1
  324.9 204.5 %all-reduce.2.cloned.1.call-done = bf16[192,1024]{1,0:T(8,128)(2,1)} async-done(((bf16[192,1024]{1,0:T(8,128)(2,1)}), bf16[192,1024]{1,0:T(8,128)(2,1)}) %all-reduce.2.cloned.1.call-update) | async-done | bytes 393232 | tf_op jit(solution)/shard_map/psum | solution.py:114
  529.4 2.0 convert_multiply_fusion
  532.2 92.3 %reduce-scatter.2.cloned.1.call-done = bf16[128,1024]{1,0:T(8,128)(2,1)} async-done(((bf16[2048,1024]{1,0:T(8,128)(2,1)}), bf16[128,1024]{1,0:T(8,128)(2,1)}) %reduce-scatter.2.cloned.1.call-update) | async-done | bytes 262160 | tf_op jit(solution)/shard_map/reduce_scatter | solution.py:101
  (84 shorter events, 34.3 us)
Async XLA Ops:
  7.2 153.0 %copy-start = (bf16[192,1024]{1,0:T(8,128)(2,1)S(1)}, bf16[192,1024]{1,0:T(8,128)(2,1)}, u32[]{:S(2)}) copy-start(bf16[192,1024]{1,0:T(8,128)(2,1)} %param.9) | copy-start | bytes 1179652
  33.7 5.5 copy-start.3
  33.7 126.5 %all-to-all-start = ((bf16[16,128,1024]{2,1,0:T(8,128)(2,1)}), bf16[16,128,1024]{2,1,0:T(8,128)(2,1)}, u32[]{:S(2)}, u32[]{:S(2)}) async-start(bf16[16,128,1024]{2,1,0:T(8,128)(2,1)} %stack.12), calls=%async_computation | async-start | bytes 8388608 | tf_op jit(solution)/shard_map/all_to_all | solution.py:44
  38.4 216.7 %all-gather.3.cloned.1.call-start = ((), (), s32[]{:S(2)}) async-start(), calls=%async_computation.6 | async-start | bytes 4456448 | tf_op jit(solution)/shard_map/all_gather | solution.py:110
  39.1 490.3 %all-reduce.2.cloned.1.call-start = ((), (), s32[]{:S(2)}) async-start(), calls=%async_computation.5 | async-start | bytes 786432 | tf_op jit(solution)/shard_map/psum | solution.py:114
  179.5 2.0 copy-start.1
  182.1 4.0 copy-start.2
  201.6 2.0 copy-start.1
  204.1 4.0 copy-start.2
  223.6 2.0 copy-start.1
  226.1 4.0 copy-start.2
  245.6 2.0 copy-start.1
  248.1 4.0 copy-start.2
  259.0 365.5 %reduce-scatter.2.cloned.1.call-start = ((), (), s32[]{:S(2)}) async-start(), calls=%async_computation.4 | async-start | bytes 4456448 | tf_op jit(solution)/shard_map/reduce_scatter | solution.py:101
  320.0 211.3 %all-to-all-start.1 = ((bf16[16,128,64]{1,2,0:T(8,128)(2,1)}), bf16[16,128,64]{1,2,0:T(8,128)(2,1)S(1)}, u32[]{:S(2)}, u32[]{:S(2)}) async-start(bf16[16,128,64]{1,2,0:T(8,128)(2,1)} %copy.18), calls=%async_computation.1 | async-start | bytes 524288 | tf_op jit(solution)/shard_map/all_to_all | solution.py:67
Sparse Core Ops, SparseCore 0:
  41.3 154.9 all-gather.2
  259.1 270.2 all-reduce.1
  532.8 91.6 reduce-scatter.1
